TPU v7x, 512 devices: a whole 4x8x8 slice. The times are simulated.
512 devices in a mesh: section: 4 (over x), rep: 128 (over y, z, core).
Axes of the slice: x: 4, y: 8, z: 8, core: 2. Of those that a mesh axis runs over, the one named last changes fastest.
Arguments:
- tile_features: bfloat16 [256, 16, 16, 512], P('rep'), may hold values from -6 to 6
- patches: bfloat16 [256, 16, 16, 768], P('rep'), may hold values from -6 to 6
- det_kernel: float32 [4, 7, 7, 512], P('section'), may hold values from -0.875 to 0.875
- det_gain: float32 [4, 512], P('section'), may hold values from 0.1 to 1.9
- det_in: bfloat16 [4, 512, 2048], P('section', None, 'rep'), may hold values from -0.25 to 0.25
- det_out: bfloat16 [4, 2048, 512], P('section', 'rep'), may hold values from -0.125 to 0.125
- det_scale: float32 [4, 512], P('section'), may hold values from 0.3 to 1.5
- cls_embed: bfloat16 [768, 1024], P(None, 'section'), may hold values from -0.21875 to 0.21875
- cls_merge: bfloat16 [512, 1024], P(None, 'section'), may hold values from -0.25 to 0.25
- cls_pos: bfloat16 [196, 1024], P(None, 'section'), may hold values from -3 to 3
- cls_qkv: bfloat16 [1024, 3, 512], P(None, None, 'section'), may hold values from -1.5 to 1.5
- cls_out: bfloat16 [512, 1024], P('section'), may hold values from -0.25 to 0.25
- cls_gain: float32 [2, 1024], replicated, may hold values from 0.1 to 1.9
- crop_plan: int32 [128, 4, 3, 3], P('rep'), may hold values from 0 to 2, as said below
- slot_from: int32 [128, 4], P('rep'), may hold values from 0 to 3, as said below
Outputs:
- crop_class: float32 [128, 4, 1024], P('rep', 'section')
Inputs may be any that keep to these rules, and one draw needn't show every extreme that they name: `crop_plan`: each entry is a micro-batch below 2 followed by a top and a left patch offset of 0 to 2; records that no slot names are arbitrary. `slot_from`: 0 marks an empty slot, 1 a crop from the replica one index lower, 2 the replica's own, 3 one from the replica one index higher; the first replica never has 1 and the last never has 3.
All inputs are finite; a program needn't handle non-finite values.
Results may differ from a plain program's by a relative error of at most 0.004.
Values may be sent and summed in bfloat16 or wider, within the bound.
No kernel may reach another device: no remote copies, remote signals or barrier semaphores. Data moves between devices by JAX's collectives and lax.ppermute only.
A program may use at most 64 MiB of HBM per device.

v0:
```python
import math
import jax
import jax.numpy as jnp
from jax import lax
from jax.sharding import PartitionSpec as P

HEAD_DIM = 64
TILE = 16
CROP = 14
epsilon = 1e-06


def passed_along(block, axis, distance):
    devices = range(lax.axis_size(axis))
    route = [(i - distance, i) for i in devices if i - distance in devices]
    return lax.ppermute(block, axis, route)


def spread(value, axis, source):
    kept = jnp.where(lax.axis_index(axis) == source, value, 0).astype(value.dtype)
    return lax.psum(kept, axis)


def padded_2(block, sides, width):
    for axis, dim in sides:
        count = lax.axis_size(axis)
        forward = [(i, i + 1) for i in range(count - 1)]
        backward = [(target, source) for source, target in forward]
        low = lax.ppermute(
            lax.slice_in_dim(block, block.shape[dim] - width, None, axis=dim), axis, forward
        )
        high = lax.ppermute(lax.slice_in_dim(block, 0, width, axis=dim), axis, backward)
        block = jnp.concatenate([low, block, high], axis=dim)
    return block


def layer_norm(values, gain_row):
    row_mean = jnp.mean(values, axis=-1, keepdims=True)
    centred = values - row_mean
    row_var = jnp.mean(centred * centred, axis=-1, keepdims=True)
    return centred * lax.rsqrt(row_var + epsilon) * gain_row


def detector_block(tile_rows, kernel, gain_row, in_weight, out_weight, scale_row):
    widened = tile_rows.astype(jnp.float32)
    padded = jnp.pad(widened, ((3, 3), (3, 3), (0, 0)))
    conv = jnp.zeros_like(widened)
    for row_shift in range(7):
        for col_shift in range(7):
            conv = (
                conv
                + padded[row_shift : row_shift + TILE, col_shift : col_shift + TILE]
                * kernel[row_shift, col_shift]
            )
    normed = layer_norm(conv, gain_row).astype(jnp.bfloat16).reshape(TILE * TILE, -1)
    hidden = jax.nn.gelu(jnp.dot(normed, in_weight, preferred_element_type=jnp.float32)).astype(
        jnp.bfloat16
    )
    update = jnp.dot(hidden, out_weight, preferred_element_type=jnp.float32).reshape(widened.shape)
    return (widened + scale_row * update).astype(jnp.bfloat16)


def per_device(
    tile_features,
    patches,
    det_kernel,
    det_gain,
    det_in,
    det_out,
    det_scale,
    cls_embed,
    cls_merge,
    cls_pos,
    cls_qkv,
    cls_out,
    cls_gain,
    crop_plan,
    slot_from,
):
    sections = lax.axis_size("section")
    section_num = lax.axis_index("section")
    micro_count = tile_features.shape[0]
    in_whole, out_whole = (
        lax.all_gather(det_in, "rep", axis=2, tiled=True),
        lax.all_gather(det_out, "rep", axis=1, tiled=True),
    )
    kernel = det_kernel[0]
    gain_row = det_gain[0]
    scale_row = det_scale[0]
    in_weight = in_whole[0]
    out_weight = out_whole[0]

    def run_block(operand_tile):
        return detector_block(operand_tile, kernel, gain_row, in_weight, out_weight, scale_row)

    def skip_block(operand_tile):
        return jnp.zeros_like(operand_tile)

    def tick(tick_index, loop_state):
        incoming, finals = loop_state
        micro_num = tick_index - section_num
        is_valid = (micro_num >= 0) & (micro_num < micro_count)
        clipped = jnp.clip(micro_num, 0, micro_count - 1)
        fresh_tile = lax.dynamic_index_in_dim(tile_features, clipped, 0, keepdims=False)
        operand = jnp.where(section_num == 0, fresh_tile, incoming)
        result = lax.cond(is_valid, run_block, skip_block, operand)
        stored = lax.dynamic_update_index_in_dim(finals, result, clipped, 0)
        finals = jnp.where(is_valid & (section_num == sections - 1), stored, finals)
        incoming = passed_along(result, "section", 1)
        return (incoming, finals)

    start_state = (
        jnp.zeros(tile_features.shape[1:], jnp.bfloat16),
        jnp.zeros(tile_features.shape, jnp.bfloat16),
    )
    unused_tile, finals = lax.fori_loop(0, micro_count + sections - 1, tick, start_state)
    finals = spread(finals, "section", sections - 1)
    pixel_width = patches.shape[3]
    feat_width = finals.shape[3]
    full_width = cls_gain.shape[1]
    local_width = cls_embed.shape[1]
    local_heads = cls_qkv.shape[2] // HEAD_DIM
    qkv_flat = cls_qkv.reshape(cls_qkv.shape[0], -1)
    gain_first = lax.dynamic_slice_in_dim(cls_gain[0], section_num * local_width, local_width)
    slot_plan = crop_plan[0]
    source = lax.dynamic_index_in_dim(slot_from[0], section_num, 0, keepdims=False)
    zero_index = jnp.int32(0)

    def cut_crop(record):
        pixel_rows = lax.dynamic_slice(
            patches, (record[0], record[1], record[2], zero_index), (1, CROP, CROP, pixel_width)
        ).reshape(CROP * CROP, pixel_width)
        feat_rows = lax.dynamic_slice(
            finals, (record[0], record[1], record[2], zero_index), (1, CROP, CROP, feat_width)
        ).reshape(CROP * CROP, feat_width)
        return (pixel_rows, feat_rows)

    pixel_rows, feat_rows = jax.vmap(cut_crop)(slot_plan.reshape(-1, 3))
    count = pixel_rows.shape[0]
    widened = (
        jnp.einsum("crp,pd->crd", pixel_rows, cls_embed, preferred_element_type=jnp.float32)
        + jnp.einsum("crp,pd->crd", feat_rows, cls_merge, preferred_element_type=jnp.float32)
        + cls_pos.astype(jnp.float32)[None]
    )
    row_sum, row_square = lax.psum(
        (jnp.sum(widened, axis=-1), jnp.sum(widened * widened, axis=-1)), "section"
    )
    row_mean = row_sum / full_width
    row_var = row_square / full_width - row_mean * row_mean
    attn_part = (
        (widened - row_mean[..., None]) * lax.rsqrt(row_var[..., None] + epsilon) * gain_first
    ).astype(jnp.bfloat16)
    attn_in = lax.all_gather(attn_part, "section", axis=2, tiled=True)
    qkv = jnp.einsum("crd,de->cre", attn_in, qkv_flat, preferred_element_type=jnp.float32).astype(
        jnp.bfloat16
    )
    qkv = qkv.reshape(count, CROP * CROP, 3, local_heads, HEAD_DIM)
    query_rows = qkv[:, :, 0]
    key_rows = qkv[:, :, 1]
    value_rows = qkv[:, :, 2]
    scores = jnp.einsum(
        "cqhd,ckhd->chqk", query_rows, key_rows, preferred_element_type=jnp.float32
    ) * (1.0 / math.sqrt(HEAD_DIM))
    top_score = jnp.max(scores, axis=-1, keepdims=True)
    weights = jnp.exp(scores - top_score)
    probs = (weights / jnp.sum(weights, axis=-1, keepdims=True)).astype(jnp.bfloat16)
    context = jnp.einsum(
        "chqk,ckhd->cqhd", probs, value_rows, preferred_element_type=jnp.float32
    ).astype(jnp.bfloat16)
    context_mean = jnp.mean(context.reshape(count, CROP * CROP, -1).astype(jnp.float32), axis=1)
    context_term = jnp.dot(
        context_mean, cls_out.astype(jnp.float32), precision=lax.Precision.HIGHEST
    )
    token_mean = jnp.mean(widened, axis=1)
    placed = lax.dynamic_update_slice_in_dim(
        jnp.zeros((count, full_width), jnp.float32), token_mean, section_num * local_width, 1
    )
    terms = (placed + context_term).reshape(sections, -1)
    pooled = lax.psum_scatter(terms, "section", scatter_dimension=0, tiled=True).reshape(
        -1, full_width
    )
    results = layer_norm(pooled, cls_gain[1])
    outgoing_results = jnp.stack([results[0], results[2]], axis=0)
    extended_results = padded_2(outgoing_results, (("rep", 0),), 1)
    result = jnp.where(
        source == 1, extended_results[0], jnp.where(source == 3, extended_results[3], results[1])
    )
    result = jnp.where(source == 0, jnp.zeros_like(result), result)
    return result[None, None, :]


def solution(mesh):
    return jax.shard_map(
        per_device,
        mesh=mesh,
        in_specs=(
            P("rep", None, None, None),
            P("rep", None, None, None),
            P("section", None, None, None),
            P("section", None),
            P("section", None, "rep"),
            P("section", "rep", None),
            P("section", None),
            P(None, "section"),
            P(None, "section"),
            P(None, "section"),
            P(None, None, "section"),
            P("section", None),
            P(),
            P("rep", None, None, None),
            P("rep", None),
        ),
        out_specs=P("rep", "section", None),
        check_vma=False,
    )
```

profile of v0, /device:TPU:32, one launch (start us, length us, event | category | flops | bytes accessed | tf_op | source)
XLA Modules:
  0.0 480.8 jit_solution(15910834706224890067)
XLA Ops:
  8.1 0.8 copy.37
  9.0 0.9 copy.64
  9.9 52.1 %while.18 = (s32[]{:T(128)}, bf16[2,16,16,768]{3,2,1,0:T(8,128)(2,1)}, s32[12,4]{0,1:T(4,128)S(1)}, bf16[12,1,14,14,768]{4,3,2,1,0:T(8,128)(2,1)}, s32[]{:T(128)}) while((s32[]{:T(128)}, bf16[2,16,16,768]{3,2,1,0:T(8,128)(2,1)}, s32[12,4]{0,1:T(4,128)S(1)}, bf16[12,1,14,14,768]{4,3,2,1,0:T(8,128)(2,1)}, s32[]{:T(128)}) %tuple.126), condition=%wide.while_cond, body=%wide.while_body.sunk | while | flops 2 | bytes 690297 | solution.py:130
  10.6 3.7 bitcast_dynamic-update-slice_fusion.2
  14.9 3.7 bitcast_dynamic-update-slice_fusion.2
  19.2 3.7 bitcast_dynamic-update-slice_fusion.2
  23.6 3.7 bitcast_dynamic-update-slice_fusion.2
  27.9 3.7 bitcast_dynamic-update-slice_fusion.2
  32.3 3.7 bitcast_dynamic-update-slice_fusion.2
  36.6 3.7 bitcast_dynamic-update-slice_fusion.2
  41.0 3.7 bitcast_dynamic-update-slice_fusion.2
  45.3 3.7 bitcast_dynamic-update-slice_fusion.2
  49.6 3.7 bitcast_dynamic-update-slice_fusion.2
  54.0 3.7 bitcast_dynamic-update-slice_fusion.2
  58.3 3.7 bitcast_dynamic-update-slice_fusion.2
  62.0 34.7 %all-gather.4.cloned.1.call-done = bf16[1,512,2048]{1,2,0:T(8,128)(2,1)} async-done(((bf16[1,512,16]{1,2,0:T(8,128)(2,1)}), bf16[1,512,2048]{1,2,0:T(8,128)(2,1)}) %all-gather.4.cloned.1.call-update) | async-done | bytes 2097168 | tf_op jit(solution)/shard_map/all_gather | solution.py:84
  96.7 4.0 copy.39
  100.7 79.0 %all-gather.6.cloned.1.call-done = bf16[1,2048,512]{2,1,0:T(8,128)(2,1)} async-done(((bf16[1,16,512]{2,1,0:T(8,128)(2,1)}), bf16[1,2048,512]{2,1,0:T(8,128)(2,1)}) %all-gather.6.cloned.1.call-update) | async-done | bytes 2097168 | tf_op jit(solution)/shard_map/all_gather | solution.py:85
  179.7 84.6 %while.17 = (s32[]{:T(128)}, bf16[16,16,512]{2,1,0:T(8,128)(2,1)S(1)}, bf16[2,16,16,512]{3,2,1,0:T(8,128)(2,1)S(1)}, s32[]{:T(128)}, pred[]{:T(512)}, /*index=5*...) while((s32[]{:T(128)}, ...), condition=%wide.region_5.6_spmd, body=%wide.region_0.5_spmd.sunk | while | flops 1093009664 | bytes 12373336 | solution.py:116
  179.8 10.3 %conditional.2 = (bf16[16,16,512]{2,1,0:T(8,128)(2,1)}, bf16[1,16,16,512]{3,2,1,0:T(8,128)(2,1)S(1)}) conditional(s32[]{:T(128)} %convert_element_type.74, () %tuple.120, (pred[]{:T(512)}, bf16[2,16,16,512]{3,2,1,0:T(8,128)(2,1)S(1)}, s32[]{:T(128)}, bf16[16,16,512]{2,1,0:T(8,128)(2,1)S(1)}, f32[1,512]{1,0:T(1,128)S(1)}, ...), branch_computations={%region_1.1_spmd, %region_2.4_spmd} | conditional | flops 1092878592 | bytes 10538005 | solution.py:106
  180.0 4.2 fusion.129
  184.6 3.8 fusion.8
  188.4 0.8 add_convert_fusion
  189.2 0.9 copy.68
  190.1 1.3 collective-permute-start
  191.5 6.5 %collective-permute-done = bf16[16,16,512]{2,1,0:T(8,128)(2,1)S(1)} collective-permute-done((bf16[16,16,512]{2,1,0:T(8,128)(2,1)}, bf16[16,16,512]{2,1,0:T(8,128)(2,1)S(1)}, u32[]{:S(2)}, u32[]{:S(2)}) %collective-permute-start) | collective-permute-done | bytes 262176 | tf_op jit(solution)/shard_map/while/body/eval_jaxpr/ppermute | solution.py:16
  198.0 10.3 %conditional.2 = (bf16[16,16,512]{2,1,0:T(8,128)(2,1)}, bf16[1,16,16,512]{3,2,1,0:T(8,128)(2,1)S(1)}) conditional(s32[]{:T(128)} %convert_element_type.74, () %tuple.120, (pred[]{:T(512)}, bf16[2,16,16,512]{3,2,1,0:T(8,128)(2,1)S(1)}, s32[]{:T(128)}, bf16[16,16,512]{2,1,0:T(8,128)(2,1)S(1)}, f32[1,512]{1,0:T(1,128)S(1)}, ...), branch_computations={%region_1.1_spmd, %region_2.4_spmd} | conditional | flops 1092878592 | bytes 10538005 | solution.py:106
  198.1 4.2 fusion.129
  202.8 3.8 fusion.8
  206.6 0.8 add_convert_fusion
  207.4 0.9 copy.68
  208.3 4.3 collective-permute-start
  212.7 5.7 %collective-permute-done = bf16[16,16,512]{2,1,0:T(8,128)(2,1)S(1)} collective-permute-done((bf16[16,16,512]{2,1,0:T(8,128)(2,1)}, bf16[16,16,512]{2,1,0:T(8,128)(2,1)S(1)}, u32[]{:S(2)}, u32[]{:S(2)}) %collective-permute-start) | collective-permute-done | bytes 262176 | tf_op jit(solution)/shard_map/while/body/eval_jaxpr/ppermute | solution.py:16
  218.4 0.7 conditional.2
  218.4 0.7 broadcast.139
  219.2 13.9 %collective-permute-start = (bf16[16,16,512]{2,1,0:T(8,128)(2,1)}, bf16[16,16,512]{2,1,0:T(8,128)(2,1)S(1)}, u32[]{:S(2)}, u32[]{:S(2)}) collective-permute-start(bf16[16,16,512]{2,1,0:T(8,128)(2,1)} %get-tuple-element.531), channel_id=1, source_target_pairs={{0,128},{128,256},{256,384},{1,129},{129,257},{257,385},{2,130},{1... | collective-permute-start | bytes 786440 | tf_op jit(solution)/shard_map/while/body/eval_jaxpr/ppermute | solution.py:16
  233.1 4.8 %collective-permute-done = bf16[16,16,512]{2,1,0:T(8,128)(2,1)S(1)} collective-permute-done((bf16[16,16,512]{2,1,0:T(8,128)(2,1)}, bf16[16,16,512]{2,1,0:T(8,128)(2,1)S(1)}, u32[]{:S(2)}, u32[]{:S(2)}) %collective-permute-start) | collective-permute-done | bytes 262176 | tf_op jit(solution)/shard_map/while/body/eval_jaxpr/ppermute | solution.py:16
  237.9 0.7 conditional.2
  237.9 0.7 broadcast.139
  238.7 4.3 collective-permute-start
  243.1 4.1 collective-permute-done
  247.2 0.7 conditional.2
  247.2 0.7 broadcast.139
  247.9 12.2 %collective-permute-start = (bf16[16,16,512]{2,1,0:T(8,128)(2,1)}, bf16[16,16,512]{2,1,0:T(8,128)(2,1)S(1)}, u32[]{:S(2)}, u32[]{:S(2)}) collective-permute-start(bf16[16,16,512]{2,1,0:T(8,128)(2,1)} %get-tuple-element.531), channel_id=1, source_target_pairs={{0,128},{128,256},{256,384},{1,129},{129,257},{257,385},{2,130},{1... | collective-permute-start | bytes 786440 | tf_op jit(solution)/shard_map/while/body/eval_jaxpr/ppermute | solution.py:16
  260.2 4.1 collective-permute-done
  264.3 1.5 broadcast_select_fusion
  266.1 6.0 %reshape.115 = bf16[12,196,768]{2,1,0:T(8,128)(2,1)} reshape(bf16[12,1,14,14,768]{4,3,2,1,0:T(8,128)(2,1)} %get-tuple-element.289) | data formatting | bytes 7225344 | tf_op jit(solution)/shard_map/vmap()/reshape | solution.py:132
  272.2 3.2 fusion.123
  275.3 52.9 %all-reduce.5.cloned.1.call-done = bf16[2,16,16,512]{3,0,2,1:T(2,128)(2,1)} async-done(((bf16[2,16,16,512]{3,0,2,1:T(2,128)(2,1)}), bf16[2,16,16,512]{3,0,2,1:T(2,128)(2,1)}) %all-reduce.5.cloned.1.call-update) | async-done | bytes 524304 | tf_op jit(solution)/shard_map/psum | solution.py:21
  328.2 12.1 %gather_fusion = bf16[12,14,14,512]{3,0,2,1:T(8,128)(2,1)} fusion(bf16[2,16,16,512]{3,0,2,1:T(2,128)(2,1)} %all-reduce.5.cloned.1.call-done, s32[12]{0:T(128)S(1)} %get-tuple-element.423), kind=kCustom, calls=%fused_computation | custom fusion | bytes 4817088 | tf_op jit(solution)/shard_map/vmap()/gather | solution.py:133
  340.3 6.5 %fusion.128 = (f32[12,256]{1,0:T(8,128)S(1)}, f32[12,196]{1,0:T(8,128)S(1)}, f32[12,196]{1,0:T(8,128)S(1)}, f32[12,196,256]{2,1,0:T(8,128)}) fusion(f32[196,256]{1,0:T(8,128)S(1)} %convert_element_type.50, f32[12,196,256]{2,1,0:T(8,128)S(1)} %fusion.123, bf16[512,256]{1,0:T(8,128)(2,1)S(1)} %copy-done.9, bf16[12,196,512]{2,0,1:T(8,128)(2,1)} %bitcast.131), kind=kOutput, calls=%fused_computation.214 | convolution fusion | flops 620167552 | bytes 7719296 | tf_op jit(solution)/shard_map/crp,pd->crd/dot_general | solution.py:142
  346.7 16.1 %all-reduce.2 = (f32[12,196]{1,0:T(8,128)S(1)}, f32[12,196]{1,0:T(8,128)S(1)}) all-reduce(f32[12,196]{1,0:T(8,128)S(1)} %get-tuple-element.327, f32[12,196]{1,0:T(8,128)S(1)} %get-tuple-element.328), channel_id=1, replica_groups=mesh['section'=4,'rep'=128] {'section'}, use_global_device_ids=true, to_apply=%region_10.11 | all-reduce | flops 4704 | bytes 37632 | tf_op jit(solution)/shard_map/psum | solution.py:145
  362.8 3.0 multiply_convert_fusion.1
  366.2 1.3 dynamic-slice.12
  367.5 61.6 %all-gather.8.cloned.1.call-done = bf16[12,196,1024]{2,1,0:T(8,128)(2,1)} async-done(((bf16[12,196,256]{2,1,0:T(8,128)(2,1)}), bf16[12,196,1024]{2,1,0:T(8,128)(2,1)}) %all-gather.8.cloned.1.call-update) | async-done | bytes 4816912 | tf_op jit(solution)/shard_map/all_gather | solution.py:153
  429.1 6.4 %convolution_convert_fusion = bf16[12,196,384]{2,1,0:T(8,128)(2,1)} fusion(bf16[12,196,1024]{2,1,0:T(8,128)(2,1)} %all-gather.8.cloned.1.call-done, bf16[1024,384,1]{0,1,2:T(8,128)(2,1)S(1)} %bitcast.133), kind=kOutput, calls=%fused_computation.181 | convolution fusion | flops 1850591232 | bytes 7409664 | tf_op jit(solution)/shard_map/crd,de->cre/dot_general | solution.py:154
  435.6 2.7 copy.44
  438.3 0.8 fusion.122
  439.1 4.1 fusion.137
  443.3 0.8 convert_reduce_fusion
  444.5 16.7 %all-reduce.1 = f32[4,3072]{1,0:T(4,128)S(1)} all-reduce(f32[4,3072]{1,0:T(4,128)S(1)} %reshape.119), channel_id=2, replica_groups=mesh['section'=4,'rep'=128] {'section'}, use_global_device_ids=true, to_apply=%region_15.16.clone | all-reduce | flops 12288 | bytes 98304
  462.3 1.9 collective-permute-start.1
  464.3 7.0 %collective-permute-start.2 = (f32[1,1024]{1,0:T(1,128)S(1)}, f32[1,1024]{1,0:T(1,128)S(1)}, u32[]{:S(2)}, u32[]{:S(2)}) collective-permute-start(f32[1,1024]{1,0:T(1,128)S(1)} %get-tuple-element.417), channel_id=1, source_target_pairs={{1,0},{2,1},{3,2},{4,3},{5,4},{6,5},{7,6},{8,7},{9,8},{10,9},{11,1... | collective-permute-start | bytes 12296 | tf_op jit(solution)/shard_map/ppermute | solution.py:32
  473.1 1.2 fusion.126
  (104 shorter events, 14.0 us)
Async XLA Ops:
  6.5 265.6 %copy-start = (bf16[768,256]{1,0:T(8,128)(2,1)S(1)}, bf16[768,256]{1,0:T(8,128)(2,1)}, u32[]{:S(2)}) copy-start(bf16[768,256]{1,0:T(8,128)(2,1)} %param.26) | copy-start | bytes 1179652
  6.5 90.1 %all-gather.4.cloned.1.call-start = ((), (), s32[]{:S(2)}) async-start(), calls=%async_computation | async-start | bytes 2113536 | tf_op jit(solution)/shard_map/all_gather | solution.py:84
  7.3 172.4 %all-gather.6.cloned.1.call-start = ((), (), s32[]{:S(2)}) async-start(), calls=%async_computation.1 | async-start | bytes 2113536 | tf_op jit(solution)/shard_map/all_gather | solution.py:85
  8.0 320.2 %all-reduce.5.cloned.1.call-start = ((), (), s32[]{:S(2)}) async-start(), calls=%async_computation.2 | async-start | bytes 1048576 | tf_op jit(solution)/shard_map/psum | solution.py:21
  96.7 83.1 %copy-start.1 = (bf16[2,16,16,512]{3,2,1,0:T(8,128)(2,1)S(1)}, bf16[2,16,16,512]{3,2,1,0:T(8,128)(2,1)}, u32[]{:S(2)}) copy-start(bf16[2,16,16,512]{3,2,1,0:T(8,128)(2,1)} %param.19) | copy-start | bytes 1572868
  96.7 83.1 %copy-start.5 = (f32[1,512]{1,0:T(1,128)S(1)}, f32[1,512]{1,0:T(1,128)}, u32[]{:S(2)}) copy-start(f32[1,512]{1,0:T(1,128)} %param.25) | copy-start | bytes 6148
  96.7 83.1 %copy-start.6 = (f32[1,512]{1,0:T(1,128)S(1)}, f32[1,512]{1,0:T(1,128)}, u32[]{:S(2)}) copy-start(f32[1,512]{1,0:T(1,128)} %param.22) | copy-start | bytes 6148
  179.7 86.3 %copy-start.7 = (f32[2,1024]{1,0:T(2,128)S(1)}, f32[2,1024]{1,0:T(2,128)}, u32[]{:S(2)}) copy-start(f32[2,1024]{1,0:T(2,128)} %param.31) | copy-start | bytes 24580
  190.1 7.9 %collective-permute-start = (bf16[16,16,512]{2,1,0:T(8,128)(2,1)}, bf16[16,16,512]{2,1,0:T(8,128)(2,1)S(1)}, u32[]{:S(2)}, u32[]{:S(2)}) collective-permute-start(bf16[16,16,512]{2,1,0:T(8,128)(2,1)} %get-tuple-element.531), channel_id=1, source_target_pairs={{0,128},{128,256},{256,384},{1,129},{129,257},{257,385},{2,130},{1... | collective-permute-start | bytes 786440 | tf_op jit(solution)/shard_map/while/body/eval_jaxpr/ppermute | solution.py:16
  208.3 10.1 %collective-permute-start = (bf16[16,16,512]{2,1,0:T(8,128)(2,1)}, bf16[16,16,512]{2,1,0:T(8,128)(2,1)S(1)}, u32[]{:S(2)}, u32[]{:S(2)}) collective-permute-start(bf16[16,16,512]{2,1,0:T(8,128)(2,1)} %get-tuple-element.531), channel_id=1, source_target_pairs={{0,128},{128,256},{256,384},{1,129},{129,257},{257,385},{2,130},{1... | collective-permute-start | bytes 786440 | tf_op jit(solution)/shard_map/while/body/eval_jaxpr/ppermute | solution.py:16
  219.2 18.8 %collective-permute-start = (bf16[16,16,512]{2,1,0:T(8,128)(2,1)}, bf16[16,16,512]{2,1,0:T(8,128)(2,1)S(1)}, u32[]{:S(2)}, u32[]{:S(2)}) collective-permute-start(bf16[16,16,512]{2,1,0:T(8,128)(2,1)} %get-tuple-element.531), channel_id=1, source_target_pairs={{0,128},{128,256},{256,384},{1,129},{129,257},{257,385},{2,130},{1... | collective-permute-start | bytes 786440 | tf_op jit(solution)/shard_map/while/body/eval_jaxpr/ppermute | solution.py:16
  238.7 8.5 %collective-permute-start = (bf16[16,16,512]{2,1,0:T(8,128)(2,1)}, bf16[16,16,512]{2,1,0:T(8,128)(2,1)S(1)}, u32[]{:S(2)}, u32[]{:S(2)}) collective-permute-start(bf16[16,16,512]{2,1,0:T(8,128)(2,1)} %get-tuple-element.531), channel_id=1, source_target_pairs={{0,128},{128,256},{256,384},{1,129},{129,257},{257,385},{2,130},{1... | collective-permute-start | bytes 786440 | tf_op jit(solution)/shard_map/while/body/eval_jaxpr/ppermute | solution.py:16
  247.9 16.4 %collective-permute-start = (bf16[16,16,512]{2,1,0:T(8,128)(2,1)}, bf16[16,16,512]{2,1,0:T(8,128)(2,1)S(1)}, u32[]{:S(2)}, u32[]{:S(2)}) collective-permute-start(bf16[16,16,512]{2,1,0:T(8,128)(2,1)} %get-tuple-element.531), channel_id=1, source_target_pairs={{0,128},{128,256},{256,384},{1,129},{129,257},{257,385},{2,130},{1... | collective-permute-start | bytes 786440 | tf_op jit(solution)/shard_map/while/body/eval_jaxpr/ppermute | solution.py:16
  265.8 163.3 %all-gather.8.cloned.1.call-start = ((), (), s32[]{:S(2)}) async-start(), calls=%async_computation.3 | async-start | bytes 6144000 | tf_op jit(solution)/shard_map/all_gather | solution.py:153
  266.1 6.0 %copy-start.4 = (bf16[196,256]{1,0:T(8,128)(2,1)S(1)}, bf16[196,256]{1,0:T(8,128)(2,1)}, u32[]{:S(2)}) copy-start(bf16[196,256]{1,0:T(8,128)(2,1)} %param.28) | copy-start | bytes 301060
  328.2 12.1 %copy-start.9 = (bf16[512,256]{1,0:T(8,128)(2,1)S(1)}, bf16[512,256]{1,0:T(8,128)(2,1)}, u32[]{:S(2)}) copy-start(bf16[512,256]{1,0:T(8,128)(2,1)} %param.27) | copy-start | bytes 786436
  362.8 3.1 copy-start.2
  443.3 1.0 copy-start.3
  443.3 28.0 %copy-start.8 = (s32[1,4]{1,0:T(1,128)S(1)}, s32[1,4]{1,0:T(1,128)}, u32[]{:S(2)}) copy-start(s32[1,4]{1,0:T(1,128)} %param.33) | copy-start | bytes 52
  462.3 10.8 %collective-permute-start.1 = (f32[1,1024]{1,0:T(1,128)S(1)}, f32[1,1024]{1,0:T(1,128)S(1)}, u32[]{:S(2)}, u32[]{:S(2)}) collective-permute-start(f32[1,1024]{1,0:T(1,128)S(1)} %get-tuple-element.418), channel_id=1, source_target_pairs={{0,1},{1,2},{2,3},{3,4},{4,5},{5,6},{6,7},{7,8},{8,9},{9,10},{10,1... | collective-permute-start | bytes 12296 | tf_op jit(solution)/shard_map/ppermute | solution.py:29
  464.3 8.9 %collective-permute-start.2 = (f32[1,1024]{1,0:T(1,128)S(1)}, f32[1,1024]{1,0:T(1,128)S(1)}, u32[]{:S(2)}, u32[]{:S(2)}) collective-permute-start(f32[1,1024]{1,0:T(1,128)S(1)} %get-tuple-element.417), channel_id=1, source_target_pairs={{1,0},{2,1},{3,2},{4,3},{5,4},{6,5},{7,6},{8,7},{9,8},{10,9},{11,1... | collective-permute-start | bytes 12296 | tf_op jit(solution)/shard_map/ppermute | solution.py:32
Sparse Core Ops, SparseCore 0:
  10.5 86.1 all-gather.3
  99.8 79.7 all-gather.5
  265.9 62.2 all-reduce.4
  366.0 63.1 all-gather.7
where the time goes:
time: 482 us; the launch traced here: 481 us
  waiting for transfers between devices  255 us (53%)
  local copies, waits for them, and re-layouts  85.6 us (18%)
  starting transfers between devices  45.1 us (9%)
  blocking collectives  32.7 us (7%)
  matrix products  25.5 us (5%)
  other arithmetic  22.2 us (5%)
  between operations  14.8 us (3%)
    all_gather x1, waiting for transfers between devices, per_device(): lax.all_gather(det_out, 'rep', axis=1, tiled=True)  79 us
    all_gather x1, waiting for transfers between devices, per_device(): attn_in = lax.all_gather(attn_part, 'section', axis=2, tiled=True)  61.6 us
    psum x1, waiting for transfers between devices, spread(): return lax.psum(kept, axis)  52.9 us
    gather x36, local copies, waits for them, and re-layouts  52 us
    ppermute x5, starting transfers between devices, passed_along(): return lax.ppermute(block, axis, route)  35.9 us
    all_gather x1, waiting for transfers between devices, per_device(): lax.all_gather(det_in, 'rep', axis=2, tiled=True)  34.7 us
    ppermute x5, waiting for transfers between devices, passed_along(): return lax.ppermute(block, axis, route)  25.1 us
    unnamed x1, blocking collectives  16.7 us
  transfers between devices with their start and end apart: 11, of which 9 were waited for; matrix products, arithmetic and copies ran while one was open for 15% of the time, Pallas kernels for 0%

commit v1 on v0

--- a/solution.py
+++ b/solution.py
@@ -150,7 +150,14 @@
     attn_part = (
         (widened - row_mean[..., None]) * lax.rsqrt(row_var[..., None] + epsilon) * gain_first
     ).astype(jnp.bfloat16)
-    attn_in = lax.all_gather(attn_part, "section", axis=2, tiled=True)
+    ring = [attn_part]
+    for hop in range(3):
+        ring.append(lax.ppermute(ring[-1], "section", [(dev, (dev + 1) % 4) for dev in range(4)]))
+    attn_in = jnp.roll(
+        jnp.concatenate(ring[::-1], axis=2),
+        (lax.axis_index("section") + 1) * ring[0].shape[2],
+        axis=2,
+    )
     qkv = jnp.einsum("crd,de->cre", attn_in, qkv_flat, preferred_element_type=jnp.float32).astype(
         jnp.bfloat16
     )

time: 482 us -> 501 us (1.039)
  local copies, waits for them, and re-layouts: 85.6 us -> 94.3 us
  waiting for transfers between devices: 255 us -> 262 us
  starting transfers between devices: 45.1 us -> 50.6 us
    ppermute x0 -> x3, waiting for transfers between devices: none -> 70.2 us  [per_device(): lax.ppermute(ring[-1], 'section', [(dev, (dev + 1) % 4) for dev in range(...]
    all_gather x1 -> x0, waiting for transfers between devices: 61.6 us -> none  [per_device(): attn_in = lax.all_gather(attn_part, 'section', axis=2, tiled=True)]
    unnamed x25 -> x35, local copies, waits for them, and re-layouts: 4.14 us -> 13.6 us
    ppermute x0 -> x3, starting transfers between devices: none -> 5.74 us  [per_device(): lax.ppermute(ring[-1], 'section', [(dev, (dev + 1) % 4) for dev in range(...]
  transfers between devices with their start and end apart: 11 -> 13, of which waited for: 9 -> 11; matrix products, arithmetic and copies ran while one was open for 15% -> 15% of each run, Pallas kernels for 0% -> 0%
where the time goes in v1:
time: 501 us; the launch traced here: 499 us
  waiting for transfers between devices  262 us (52%)
  local copies, waits for them, and re-layouts  94.3 us (19%)
  starting transfers between devices  50.6 us (10%)
  blocking collectives  30.7 us (6%)
  matrix products  23.8 us (5%)
  other arithmetic  22.1 us (4%)
  between operations  14.8 us (3%)
    all_gather x1, waiting for transfers between devices, per_device(): lax.all_gather(det_out, 'rep', axis=1, tiled=True)  78.9 us
    ppermute x3, waiting for transfers between devices, per_device(): lax.ppermute(ring[-1], 'section', [(dev, (dev + 1) % 4) for dev in range(...  70.2 us
    psum x1, waiting for transfers between devices, spread(): return lax.psum(kept, axis)  51.7 us
    gather x36, local copies, waits for them, and re-layouts  51.6 us
    ppermute x5, starting transfers between devices, passed_along(): return lax.ppermute(block, axis, route)  35.9 us
    all_gather x1, waiting for transfers between devices, per_device(): lax.all_gather(det_in, 'rep', axis=2, tiled=True)  35.1 us
    ppermute x5, waiting for transfers between devices, passed_along(): return lax.ppermute(block, axis, route)  25.1 us
    psum x1, blocking collectives, per_device(): lax.psum((jnp.sum(widened, axis=-1), jnp.sum(widened * widened, axis=-1))...  16.1 us
  transfers between devices with their start and end apart: 13, of which 11 were waited for; matrix products, arithmetic and copies ran while one was open for 15% of the time, Pallas kernels for 0%

profile of v1, /device:TPU:32, one launch (start us, length us, event | category | flops | bytes accessed | tf_op | source)
XLA Modules:
  0.0 499.2 jit_solution(12372232525587960163)
XLA Ops:
  9.0 0.9 copy.64
  9.9 51.6 %while.18 = (s32[]{:T(128)}, bf16[2,16,16,768]{3,2,1,0:T(8,128)(2,1)}, s32[12,4]{0,1:T(4,128)S(1)}, bf16[12,1,14,14,768]{4,3,2,1,0:T(8,128)(2,1)}, s32[]{:T(128)}) while((s32[]{:T(128)}, bf16[2,16,16,768]{3,2,1,0:T(8,128)(2,1)}, s32[12,4]{0,1:T(4,128)S(1)}, bf16[12,1,14,14,768]{4,3,2,1,0:T(8,128)(2,1)}, s32[]{:T(128)}) %tuple.126), condition=%wide.while_cond, body=%wide.while_body.sunk | while | flops 2 | bytes 690297 | solution.py:130
  10.6 3.6 bitcast_dynamic-update-slice_fusion.2
  14.9 3.6 bitcast_dynamic-update-slice_fusion.2
  19.2 3.6 bitcast_dynamic-update-slice_fusion.2
  23.5 3.6 bitcast_dynamic-update-slice_fusion.2
  27.8 3.6 bitcast_dynamic-update-slice_fusion.2
  32.1 3.6 bitcast_dynamic-update-slice_fusion.2
  36.4 3.7 bitcast_dynamic-update-slice_fusion.2
  40.7 3.6 bitcast_dynamic-update-slice_fusion.2
  45.0 3.6 bitcast_dynamic-update-slice_fusion.2
  49.3 3.6 bitcast_dynamic-update-slice_fusion.2
  53.6 3.6 bitcast_dynamic-update-slice_fusion.2
  57.9 3.7 bitcast_dynamic-update-slice_fusion.2
  61.6 35.1 %all-gather.3.cloned.1.call-done = bf16[1,512,2048]{1,2,0:T(8,128)(2,1)} async-done(((bf16[1,512,16]{1,2,0:T(8,128)(2,1)}), bf16[1,512,2048]{1,2,0:T(8,128)(2,1)}) %all-gather.3.cloned.1.call-update) | async-done | bytes 2097168 | tf_op jit(solution)/shard_map/all_gather | solution.py:84
  96.6 4.0 copy.39
  100.7 78.9 %all-gather.5.cloned.1.call-done = bf16[1,2048,512]{2,1,0:T(8,128)(2,1)} async-done(((bf16[1,16,512]{2,1,0:T(8,128)(2,1)}), bf16[1,2048,512]{2,1,0:T(8,128)(2,1)}) %all-gather.5.cloned.1.call-update) | async-done | bytes 2097168 | tf_op jit(solution)/shard_map/all_gather | solution.py:85
  179.7 84.6 %while.17 = (s32[]{:T(128)}, bf16[16,16,512]{2,1,0:T(8,128)(2,1)S(1)}, bf16[2,16,16,512]{3,2,1,0:T(8,128)(2,1)S(1)}, s32[]{:T(128)}, pred[]{:T(512)}, /*index=5*...) while((s32[]{:T(128)}, ...), condition=%wide.region_5.6_spmd, body=%wide.region_0.5_spmd.sunk | while | flops 1093009664 | bytes 12373336 | solution.py:116
  179.7 10.4 %conditional.2 = (bf16[16,16,512]{2,1,0:T(8,128)(2,1)}, bf16[1,16,16,512]{3,2,1,0:T(8,128)(2,1)S(1)}) conditional(s32[]{:T(128)} %convert_element_type.78, () %tuple.120, (pred[]{:T(512)}, bf16[2,16,16,512]{3,2,1,0:T(8,128)(2,1)S(1)}, s32[]{:T(128)}, bf16[16,16,512]{2,1,0:T(8,128)(2,1)S(1)}, f32[1,512]{1,0:T(1,128)S(1)}, ...), branch_computations={%region_1.1_spmd, %region_2.4_spmd} | conditional | flops 1092878592 | bytes 10538005 | solution.py:106
  179.9 4.2 fusion.135
  184.5 3.8 fusion.8
  189.2 0.9 copy.68
  190.1 1.3 collective-permute-start
  191.5 6.5 %collective-permute-done = bf16[16,16,512]{2,1,0:T(8,128)(2,1)S(1)} collective-permute-done((bf16[16,16,512]{2,1,0:T(8,128)(2,1)}, bf16[16,16,512]{2,1,0:T(8,128)(2,1)S(1)}, u32[]{:S(2)}, u32[]{:S(2)}) %collective-permute-start) | collective-permute-done | bytes 262176 | tf_op jit(solution)/shard_map/while/body/eval_jaxpr/ppermute | solution.py:16
  198.0 10.3 %conditional.2 = (bf16[16,16,512]{2,1,0:T(8,128)(2,1)}, bf16[1,16,16,512]{3,2,1,0:T(8,128)(2,1)S(1)}) conditional(s32[]{:T(128)} %convert_element_type.78, () %tuple.120, (pred[]{:T(512)}, bf16[2,16,16,512]{3,2,1,0:T(8,128)(2,1)S(1)}, s32[]{:T(128)}, bf16[16,16,512]{2,1,0:T(8,128)(2,1)S(1)}, f32[1,512]{1,0:T(1,128)S(1)}, ...), branch_computations={%region_1.1_spmd, %region_2.4_spmd} | conditional | flops 1092878592 | bytes 10538005 | solution.py:106
  198.1 4.2 fusion.135
  202.8 3.8 fusion.8
  207.4 0.9 copy.68
  208.3 4.3 collective-permute-start
  212.7 5.7 %collective-permute-done = bf16[16,16,512]{2,1,0:T(8,128)(2,1)S(1)} collective-permute-done((bf16[16,16,512]{2,1,0:T(8,128)(2,1)}, bf16[16,16,512]{2,1,0:T(8,128)(2,1)S(1)}, u32[]{:S(2)}, u32[]{:S(2)}) %collective-permute-start) | collective-permute-done | bytes 262176 | tf_op jit(solution)/shard_map/while/body/eval_jaxpr/ppermute | solution.py:16
  219.2 13.8 %collective-permute-start = (bf16[16,16,512]{2,1,0:T(8,128)(2,1)}, bf16[16,16,512]{2,1,0:T(8,128)(2,1)S(1)}, u32[]{:S(2)}, u32[]{:S(2)}) collective-permute-start(bf16[16,16,512]{2,1,0:T(8,128)(2,1)} %get-tuple-element.531), channel_id=1, source_target_pairs={{0,128},{128,256},{256,384},{1,129},{129,257},{257,385},{2,130},{1... | collective-permute-start | bytes 786440 | tf_op jit(solution)/shard_map/while/body/eval_jaxpr/ppermute | solution.py:16
  233.1 4.8 collective-permute-done
  238.7 4.3 collective-permute-start
  243.1 4.1 collective-permute-done
  248.0 12.2 %collective-permute-start = (bf16[16,16,512]{2,1,0:T(8,128)(2,1)}, bf16[16,16,512]{2,1,0:T(8,128)(2,1)S(1)}, u32[]{:S(2)}, u32[]{:S(2)}) collective-permute-start(bf16[16,16,512]{2,1,0:T(8,128)(2,1)} %get-tuple-element.531), channel_id=1, source_target_pairs={{0,128},{128,256},{256,384},{1,129},{129,257},{257,385},{2,130},{1... | collective-permute-start | bytes 786440 | tf_op jit(solution)/shard_map/while/body/eval_jaxpr/ppermute | solution.py:16
  260.3 4.1 collective-permute-done
  264.3 1.4 broadcast_select_fusion
  265.8 6.1 %reshape.115 = bf16[12,196,768]{2,1,0:T(8,128)(2,1)} reshape(bf16[12,1,14,14,768]{4,3,2,1,0:T(8,128)(2,1)} %get-tuple-element.289) | data formatting | bytes 7225344 | tf_op jit(solution)/shard_map/vmap()/reshape | solution.py:132
  272.0 4.6 fusion.128
  276.6 51.7 %all-reduce.5.cloned.1.call-done = bf16[2,16,16,512]{3,0,2,1:T(2,128)(2,1)} async-done(((bf16[2,16,16,512]{3,0,2,1:T(2,128)(2,1)}), bf16[2,16,16,512]{3,0,2,1:T(2,128)(2,1)}) %all-reduce.5.cloned.1.call-update) | async-done | bytes 524304 | tf_op jit(solution)/shard_map/psum | solution.py:21
  328.3 11.7 %gather_fusion = bf16[12,14,14,512]{3,0,2,1:T(8,128)(2,1)} fusion(bf16[2,16,16,512]{3,0,2,1:T(2,128)(2,1)} %all-reduce.5.cloned.1.call-done, s32[12]{0:T(128)S(1)} %get-tuple-element.423), kind=kCustom, calls=%fused_computation | custom fusion | bytes 4817088 | tf_op jit(solution)/shard_map/vmap()/gather | solution.py:133
  340.0 5.8 %fusion.134 = (f32[12,256]{1,0:T(8,128)S(1)}, f32[12,196]{1,0:T(8,128)S(1)}, f32[12,196]{1,0:T(8,128)S(1)}, f32[12,196,256]{2,1,0:T(8,128)S(1)}) fusion(f32[196,256]{1,0:T(8,128)S(1)} %convert_element_type.50, f32[12,196,256]{2,1,0:T(8,128)} %fusion.128, bf16[512,256]{1,0:T(8,128)(2,1)S(1)} %copy-done.11, bf16[12,196,512]{2,0,1:T(8,128)(2,1)} %bitcast.130), kind=kOutput, calls=%fused_computation.225 | convolution fusion | flops 620167552 | bytes 7719296 | tf_op jit(solution)/shard_map/crp,pd->crd/dot_general | solution.py:142
  345.8 16.1 %all-reduce.2 = (f32[12,196]{1,0:T(8,128)S(1)}, f32[12,196]{1,0:T(8,128)S(1)}) all-reduce(f32[12,196]{1,0:T(8,128)S(1)} %get-tuple-element.327, f32[12,196]{1,0:T(8,128)S(1)} %get-tuple-element.328), channel_id=1, replica_groups=mesh['section'=4,'rep'=128] {'section'}, use_global_device_ids=true, to_apply=%region_10.11 | all-reduce | flops 4704 | bytes 37632 | tf_op jit(solution)/shard_map/psum | solution.py:145
  362.8 1.9 collective-permute-start.1
  364.7 25.1 %collective-permute-done.1 = bf16[12,196,256]{2,1,0:T(8,128)(2,1)S(1)} collective-permute-done((bf16[12,196,256]{2,1,0:T(8,128)(2,1)S(1)}, bf16[12,196,256]{2,1,0:T(8,128)(2,1)S(1)}, u32[]{:S(2)}, u32[]{:S(2)}) %collective-permute-start.1) | collective-permute-done | bytes 1204256 | tf_op jit(solution)/shard_map/ppermute | solution.py:155
  389.8 1.1 copy-done.1
  390.9 1.9 collective-permute-start.2
  392.8 25.1 %collective-permute-done.2 = bf16[12,196,256]{2,1,0:T(8,128)(2,1)} collective-permute-done((bf16[12,196,256]{2,1,0:T(8,128)(2,1)S(1)}, bf16[12,196,256]{2,1,0:T(8,128)(2,1)}, u32[]{:S(2)}, u32[]{:S(2)}) %collective-permute-start.2) | collective-permute-done | bytes 1204256 | tf_op jit(solution)/shard_map/ppermute | solution.py:155
  417.9 1.9 collective-permute-start.3
  419.8 2.3 copy.42
  422.1 1.3 dynamic-slice.12
  423.4 20.0 %collective-permute-done.3 = bf16[12,196,256]{2,1,0:T(8,128)(2,1)} collective-permute-done((bf16[12,196,256]{2,1,0:T(8,128)(2,1)}, bf16[12,196,256]{2,1,0:T(8,128)(2,1)}, u32[]{:S(2)}, u32[]{:S(2)}) %collective-permute-start.3) | collective-permute-done | bytes 1204256 | tf_op jit(solution)/shard_map/ppermute | solution.py:155
  443.5 1.4 constant_dynamic-update-slice_fusion.7
  444.9 1.5 constant_dynamic-update-slice_fusion.6
  446.5 1.1 constant_dynamic-update-slice_fusion.4
  447.6 1.4 constant_dynamic-update-slice_fusion.3
  449.1 1.5 constant_dynamic-update-slice_fusion.2
  451.9 3.9 fusion.121
  455.8 2.7 copy.44
  459.4 4.1 fusion.143
  464.7 14.7 %all-reduce.1 = f32[4,3072]{1,0:T(4,128)S(1)} all-reduce(f32[4,3072]{1,0:T(4,128)S(1)} %reshape.119), channel_id=2, replica_groups=mesh['section'=4,'rep'=128] {'section'}, use_global_device_ids=true, to_apply=%region_15.16.clone | all-reduce | flops 12288 | bytes 98304
  480.5 1.9 collective-permute-start.4
  482.4 7.0 %collective-permute-start.5 = (f32[1,1024]{1,0:T(1,128)S(1)}, f32[1,1024]{1,0:T(1,128)S(1)}, u32[]{:S(2)}, u32[]{:S(2)}) collective-permute-start(f32[1,1024]{1,0:T(1,128)S(1)} %get-tuple-element.417), channel_id=1, source_target_pairs={{1,0},{2,1},{3,2},{4,3},{5,4},{6,5},{7,6},{8,7},{9,8},{10,9},{11,1... | collective-permute-start | bytes 12296 | tf_op jit(solution)/shard_map/ppermute | solution.py:32
  491.4 1.2 fusion.131
  (119 shorter events, 24.3 us)
Async XLA Ops:
  6.5 265.4 %copy-start = (bf16[768,256]{1,0:T(8,128)(2,1)S(1)}, bf16[768,256]{1,0:T(8,128)(2,1)}, u32[]{:S(2)}) copy-start(bf16[768,256]{1,0:T(8,128)(2,1)} %param.26) | copy-start | bytes 1179652
  6.5 90.1 %all-gather.3.cloned.1.call-start = ((), (), s32[]{:S(2)}) async-start(), calls=%async_computation | async-start | bytes 2113536 | tf_op jit(solution)/shard_map/all_gather | solution.py:84
  7.3 172.3 %all-gather.5.cloned.1.call-start = ((), (), s32[]{:S(2)}) async-start(), calls=%async_computation.1 | async-start | bytes 2113536 | tf_op jit(solution)/shard_map/all_gather | solution.py:85
  8.0 320.3 %all-reduce.5.cloned.1.call-start = ((), (), s32[]{:S(2)}) async-start(), calls=%async_computation.2 | async-start | bytes 1048576 | tf_op jit(solution)/shard_map/psum | solution.py:21
  96.6 83.1 %copy-start.3 = (bf16[2,16,16,512]{3,2,1,0:T(8,128)(2,1)S(1)}, bf16[2,16,16,512]{3,2,1,0:T(8,128)(2,1)}, u32[]{:S(2)}) copy-start(bf16[2,16,16,512]{3,2,1,0:T(8,128)(2,1)} %param.19) | copy-start | bytes 1572868
  96.6 83.1 %copy-start.7 = (f32[1,512]{1,0:T(1,128)S(1)}, f32[1,512]{1,0:T(1,128)}, u32[]{:S(2)}) copy-start(f32[1,512]{1,0:T(1,128)} %param.25) | copy-start | bytes 6148
  96.6 83.1 %copy-start.8 = (f32[1,512]{1,0:T(1,128)S(1)}, f32[1,512]{1,0:T(1,128)}, u32[]{:S(2)}) copy-start(f32[1,512]{1,0:T(1,128)} %param.22) | copy-start | bytes 6148
  179.7 86.1 %copy-start.9 = (f32[2,1024]{1,0:T(2,128)S(1)}, f32[2,1024]{1,0:T(2,128)}, u32[]{:S(2)}) copy-start(f32[2,1024]{1,0:T(2,128)} %param.31) | copy-start | bytes 24580
  190.1 7.9 %collective-permute-start = (bf16[16,16,512]{2,1,0:T(8,128)(2,1)}, bf16[16,16,512]{2,1,0:T(8,128)(2,1)S(1)}, u32[]{:S(2)}, u32[]{:S(2)}) collective-permute-start(bf16[16,16,512]{2,1,0:T(8,128)(2,1)} %get-tuple-element.531), channel_id=1, source_target_pairs={{0,128},{128,256},{256,384},{1,129},{129,257},{257,385},{2,130},{1... | collective-permute-start | bytes 786440 | tf_op jit(solution)/shard_map/while/body/eval_jaxpr/ppermute | solution.py:16
  208.3 10.1 %collective-permute-start = (bf16[16,16,512]{2,1,0:T(8,128)(2,1)}, bf16[16,16,512]{2,1,0:T(8,128)(2,1)S(1)}, u32[]{:S(2)}, u32[]{:S(2)}) collective-permute-start(bf16[16,16,512]{2,1,0:T(8,128)(2,1)} %get-tuple-element.531), channel_id=1, source_target_pairs={{0,128},{128,256},{256,384},{1,129},{129,257},{257,385},{2,130},{1... | collective-permute-start | bytes 786440 | tf_op jit(solution)/shard_map/while/body/eval_jaxpr/ppermute | solution.py:16
  219.2 18.7 %collective-permute-start = (bf16[16,16,512]{2,1,0:T(8,128)(2,1)}, bf16[16,16,512]{2,1,0:T(8,128)(2,1)S(1)}, u32[]{:S(2)}, u32[]{:S(2)}) collective-permute-start(bf16[16,16,512]{2,1,0:T(8,128)(2,1)} %get-tuple-element.531), channel_id=1, source_target_pairs={{0,128},{128,256},{256,384},{1,129},{129,257},{257,385},{2,130},{1... | collective-permute-start | bytes 786440 | tf_op jit(solution)/shard_map/while/body/eval_jaxpr/ppermute | solution.py:16
  238.7 8.5 %collective-permute-start = (bf16[16,16,512]{2,1,0:T(8,128)(2,1)}, bf16[16,16,512]{2,1,0:T(8,128)(2,1)S(1)}, u32[]{:S(2)}, u32[]{:S(2)}) collective-permute-start(bf16[16,16,512]{2,1,0:T(8,128)(2,1)} %get-tuple-element.531), channel_id=1, source_target_pairs={{0,128},{128,256},{256,384},{1,129},{129,257},{257,385},{2,130},{1... | collective-permute-start | bytes 786440 | tf_op jit(solution)/shard_map/while/body/eval_jaxpr/ppermute | solution.py:16
  248.0 16.4 %collective-permute-start = (bf16[16,16,512]{2,1,0:T(8,128)(2,1)}, bf16[16,16,512]{2,1,0:T(8,128)(2,1)S(1)}, u32[]{:S(2)}, u32[]{:S(2)}) collective-permute-start(bf16[16,16,512]{2,1,0:T(8,128)(2,1)} %get-tuple-element.531), channel_id=1, source_target_pairs={{0,128},{128,256},{256,384},{1,129},{129,257},{257,385},{2,130},{1... | collective-permute-start | bytes 786440 | tf_op jit(solution)/shard_map/while/body/eval_jaxpr/ppermute | solution.py:16
  265.8 6.1 %copy-start.6 = (bf16[196,256]{1,0:T(8,128)(2,1)S(1)}, bf16[196,256]{1,0:T(8,128)(2,1)}, u32[]{:S(2)}) copy-start(bf16[196,256]{1,0:T(8,128)(2,1)} %param.28) | copy-start | bytes 301060
  328.3 11.7 %copy-start.11 = (bf16[512,256]{1,0:T(8,128)(2,1)S(1)}, bf16[512,256]{1,0:T(8,128)(2,1)}, u32[]{:S(2)}) copy-start(bf16[512,256]{1,0:T(8,128)(2,1)} %param.27) | copy-start | bytes 786436
  362.8 27.1 %collective-permute-start.1 = (bf16[12,196,256]{2,1,0:T(8,128)(2,1)S(1)}, bf16[12,196,256]{2,1,0:T(8,128)(2,1)S(1)}, u32[]{:S(2)}, u32[]{:S(2)}) collective-permute-start(bf16[12,196,256]{2,1,0:T(8,128)(2,1)S(1)} %multiply_convert_fusion.1), channel_id=1, source_target_pairs={{0,128},{128,256},{256,384},{384,0},{1,129},{129,257},{257,385},{3... | collective-permute-start | bytes 3612680 | tf_op jit(solution)/shard_map/ppermute | solution.py:155
  389.8 1.1 copy-start.1
  390.9 27.0 %collective-permute-start.2 = (bf16[12,196,256]{2,1,0:T(8,128)(2,1)S(1)}, bf16[12,196,256]{2,1,0:T(8,128)(2,1)}, u32[]{:S(2)}, u32[]{:S(2)}) collective-permute-start(bf16[12,196,256]{2,1,0:T(8,128)(2,1)S(1)} %collective-permute-done.1), channel_id=1, source_target_pairs={{0,128},{128,256},{256,384},{384,0},{1,129},{129,257},{257,385},{3... | collective-permute-start | bytes 3612680 | tf_op jit(solution)/shard_map/ppermute | solution.py:155
  417.9 25.6 %collective-permute-start.3 = (bf16[12,196,256]{2,1,0:T(8,128)(2,1)}, bf16[12,196,256]{2,1,0:T(8,128)(2,1)}, u32[]{:S(2)}, u32[]{:S(2)}) collective-permute-start(bf16[12,196,256]{2,1,0:T(8,128)(2,1)} %collective-permute-done.2), channel_id=1, source_target_pairs={{0,128},{128,256},{256,384},{384,0},{1,129},{129,257},{257,385},{3... | collective-permute-start | bytes 3612680 | tf_op jit(solution)/shard_map/ppermute | solution.py:155
  423.4 22.9 %copy-start.2 = (bf16[12,196,256]{2,1,0:T(8,128)(2,1)S(1)}, bf16[12,196,256]{2,1,0:T(8,128)(2,1)}, u32[]{:S(2)}) copy-start(bf16[12,196,256]{2,1,0:T(8,128)(2,1)} %copy-done.1) | copy-start | bytes 3612676
  450.7 1.1 copy-start.4
  463.5 1.0 copy-start.5
  463.5 25.9 %copy-start.10 = (s32[1,4]{1,0:T(1,128)S(1)}, s32[1,4]{1,0:T(1,128)}, u32[]{:S(2)}) copy-start(s32[1,4]{1,0:T(1,128)} %param.33) | copy-start | bytes 52
  480.5 10.9 %collective-permute-start.4 = (f32[1,1024]{1,0:T(1,128)S(1)}, f32[1,1024]{1,0:T(1,128)S(1)}, u32[]{:S(2)}, u32[]{:S(2)}) collective-permute-start(f32[1,1024]{1,0:T(1,128)S(1)} %get-tuple-element.418), channel_id=1, source_target_pairs={{0,1},{1,2},{2,3},{3,4},{4,5},{5,6},{6,7},{7,8},{8,9},{9,10},{10,1... | collective-permute-start | bytes 12296 | tf_op jit(solution)/shard_map/ppermute | solution.py:29
  482.4 8.9 %collective-permute-start.5 = (f32[1,1024]{1,0:T(1,128)S(1)}, f32[1,1024]{1,0:T(1,128)S(1)}, u32[]{:S(2)}, u32[]{:S(2)}) collective-permute-start(f32[1,1024]{1,0:T(1,128)S(1)} %get-tuple-element.417), channel_id=1, source_target_pairs={{1,0},{2,1},{3,2},{4,3},{5,4},{6,5},{7,6},{8,7},{9,8},{10,9},{11,1... | collective-permute-start | bytes 12296 | tf_op jit(solution)/shard_map/ppermute | solution.py:32
Sparse Core Ops, SparseCore 0:
  10.5 86.0 all-gather.2
  99.7 79.7 all-gather.4
  265.9 62.3 all-reduce.4
